TPU v7x, 256 devices: a whole 4x4x8 slice. The times are simulated.
256 devices in a mesh: row: 16 (over z, core), col: 16 (over y, x).
Axes of the slice: x: 4, y: 4, z: 8, core: 2. Of those that a mesh axis runs over, the one named last changes fastest.
Arguments:
- front_blocks: bfloat16 [64, 5, 512, 512], P('row'), may hold values from -0.125 to 0.125
- block_cols: int32 [64, 5], P('row'), may hold values from 0 to 63, as said below
- samples: bfloat16 [32768, 1024], P('row', 'col'), may hold values from -6 to 6
- sketch_matrix: bfloat16 [1024, 256], replicated, may hold values from -0.1875 to 0.1875
Outputs:
- leaf_bases: bfloat16 [32768, 256], P('row')
- top_transfers: bfloat16 [1024, 256], P('row')
Inputs may be any that keep to these rules, and one draw needn't show every extreme that they name: `block_cols`: each row lists 5 different block columns; the first is the row's own index, the second lies in the other half of the 64 block columns (its index differs in the highest bit).
All inputs are finite; a program needn't handle non-finite values.
Results may differ from a plain program's by a relative error of at most 0.035.
Values may be sent and summed in bfloat16 or wider, within the bound.
No kernel may reach another device: no remote copies, remote signals or barrier semaphores. Data moves between devices by JAX's collectives and lax.ppermute only.
A program may use at most 128 MiB of HBM per device.

v0:
```python
import math

import jax
import jax.numpy as jnp
from jax import lax
from jax.sharding import PartitionSpec as P


def partner_2(value, axis, stride):
    mask = 2**stride
    pairs = [(source, source ^ mask) for source in range(lax.axis_size(axis))]
    return lax.ppermute(value, axis, pairs)


def cholqr(sketch):
    highest = lax.Precision.HIGHEST
    gram_matrix = jnp.dot(sketch.T, sketch, precision=highest)
    low_factor = jnp.linalg.cholesky(gram_matrix)
    identity = jnp.eye(sketch.shape[1], dtype=sketch.dtype)
    low_inverse = jax.scipy.linalg.solve_triangular(low_factor, identity, lower=True)
    ortho_basis = jnp.dot(sketch, low_inverse.T, precision=highest)
    return (ortho_basis * math.sqrt(sketch.shape[0])).astype(jnp.bfloat16)


def off_products(all_sketched, front_blocks, block_cols, leaf_ids, top_level):
    leaf_total = all_sketched.shape[0] // front_blocks.shape[2]
    gathered_blocks = all_sketched.reshape(
        leaf_total, front_blocks.shape[2], all_sketched.shape[1]
    )[block_cols]
    products = jnp.einsum(
        "nkab,nkbc->nkac", front_blocks, gathered_blocks, preferred_element_type=jnp.float32
    )
    level_ids = jnp.arange(top_level, dtype=jnp.int32)
    outside = (
        jnp.right_shift(leaf_ids[:, None, None], level_ids[None, :, None])
        != jnp.right_shift(block_cols[:, None, :], level_ids[None, :, None])
    ).astype(jnp.float32)
    return jnp.einsum("nlk,nkac->nlac", outside, products, precision=lax.Precision.HIGHEST).astype(
        jnp.bfloat16
    )


def shards(front_blocks, block_cols, samples, sketch_matrix):
    leaf_dev = front_blocks.shape[0]
    leaf_size = front_blocks.shape[2]
    rank_size = sketch_matrix.shape[1]
    cols_dev = samples.shape[1]
    size_rows = lax.axis_size("row")
    row_index = lax.axis_index("row")
    leaf_total = leaf_dev * size_rows
    top_level = leaf_total.bit_length() - 1
    local_levels = leaf_dev.bit_length() - 1
    leaf_ids = row_index * leaf_dev + jnp.arange(leaf_dev, dtype=jnp.int32)
    local_rows = lax.dynamic_slice_in_dim(
        sketch_matrix, lax.axis_index("col") * cols_dev, cols_dev, 0
    )
    partial_sum = jnp.dot(samples, local_rows, preferred_element_type=jnp.float32)
    sketched = lax.psum(partial_sum.astype(jnp.bfloat16), "col")
    all_sketched = lax.all_gather(sketched, "row", axis=0, tiled=True)
    off_samples = off_products(all_sketched, front_blocks, block_cols, leaf_ids, top_level)
    leaf_basis = jax.vmap(cholqr)(off_samples[:, 0].astype(jnp.float32))
    carried = jnp.einsum(
        "nar,nlac->nlrc", leaf_basis, off_samples[:, 1:], preferred_element_type=jnp.float32
    )
    carried = (carried * (1.0 / math.sqrt(leaf_size))).astype(jnp.bfloat16)
    scale_pair = 1.0 / math.sqrt(2 * rank_size)
    transfer = None
    for tree_level in range(1, top_level):
        if carried.shape[0] >= 2:
            node_count = carried.shape[0] // 2
            paired = carried.reshape(node_count, 2, carried.shape[1], rank_size, rank_size)
            stacked = jnp.concatenate([paired[:, 0], paired[:, 1]], axis=2)
        else:
            swap_bit = tree_level - local_levels - 1
            is_left = jnp.right_shift(row_index, swap_bit) % 2 == 0
            partner = partner_2(carried, "row", swap_bit)
            left_part = jnp.where(is_left, carried, partner)
            right_part = jnp.where(is_left, partner, carried)
            stacked = jnp.concatenate([left_part, right_part], axis=2)
        transfer = jax.vmap(cholqr)(stacked[:, 0].astype(jnp.float32))
        if tree_level < top_level - 1:
            moved = jnp.einsum(
                "npr,nlpc->nlrc", transfer, stacked[:, 1:], preferred_element_type=jnp.float32
            )
            carried = (moved * scale_pair).astype(jnp.bfloat16)
    out_rows = 4 * rank_size // size_rows
    offset = row_index % (size_rows // 2) * out_rows
    top_rows = lax.dynamic_slice_in_dim(transfer[0], offset, out_rows, 0)
    return (leaf_basis.reshape(leaf_dev * leaf_size, rank_size), top_rows)


def solution(mesh):
    placed = (P("row", None, None, None), P("row", None), P("row", "col"), P())
    return jax.shard_map(
        shards,
        mesh=mesh,
        in_specs=placed,
        out_specs=(P("row", None), P("row", None)),
        check_vma=False,
    )
```

profile of v0, /device:TPU:1, one launch (start us, length us, event | category | flops | bytes accessed | tf_op | source)
XLA Modules:
  0.0 963.2 jit_solution(16113320740704673089)
XLA Ops:
  10.7 100.7 %all-reduce.5.cloned.1.call-done = bf16[2048,256]{0,1:T(8,128)(2,1)} async-done(((bf16[2048,256]{0,1:T(8,128)(2,1)}), bf16[2048,256]{0,1:T(8,128)(2,1)}) %all-reduce.5.cloned.1.call-update) | async-done | bytes 1048592 | tf_op jit(solution)/shard_map/psum | solution.py:58
  111.8 98.0 %all-gather.2.cloned.1.call-done = bf16[32768,256]{0,1:T(8,128)(2,1)} async-done(((bf16[2048,256]{0,1:T(8,128)(2,1)}), bf16[32768,256]{0,1:T(8,128)(2,1)}) %all-gather.2.cloned.1.call-update) | async-done | bytes 16777232 | tf_op jit(solution)/shard_map/all_gather | solution.py:59
  209.8 22.4 %copy.112 = bf16[32768,256]{1,0:T(8,128)(2,1)} copy(bf16[32768,256]{0,1:T(8,128)(2,1)} %all-gather.2.cloned.1.call-done) | data formatting | bytes 33554432 | tf_op jit(solution)/shard_map/reshape | solution.py:27
  242.0 12.5 %convolution_bitcast_fusion = f32[4,5,512,256]{2,3,1,0:T(8,128)} fusion(bf16[4,5,512,256]{3,2,1,0:T(8,128)(2,1)} %bitcast.433, bf16[4,5,512,512]{3,2,1,0:T(8,128)(2,1)} %param.7), kind=kOutput, calls=%fused_computation.17 | convolution fusion | flops 2684354560 | bytes 26214400 | tf_op jit(solution)/shard_map/nkab,nkbc->nkac/dot_general | solution.py:30
  254.6 17.1 %copy.63 = f32[4,5,512,256]{3,1,2,0:T(8,128)} copy(f32[4,5,512,256]{2,3,1,0:T(8,128)} %convolution_bitcast_fusion) | data formatting | bytes 20971520 | tf_op jit(solution)/shard_map/nkab,nkbc->nkac/dot_general | solution.py:30
  271.7 11.9 %convolution_convert_fusion = bf16[4,6,512,256]{3,1,2,0:T(8,128)(2,1)S(1)} fusion(f32[4,5,512,256]{3,1,2,0:T(8,128)} %copy.63, s32[4,5]{1,0:T(4,128)S(1)} %copy-done.11, s32[4,6]{1,0:T(4,128)S(1)} %iota_shift-right-arithmetic_fusion), kind=kOutput, calls=%fused_computation.13 | convolution fusion | flops 191889648 | bytes 16777392 | tf_op jit(solution)/shard_map/nlk,nkac->nlac/dot_general | solution.py:38
  299.7 46.9 %custom-call.47 = f32[4,128,128]{2,1,0:T(8,128)S(1)} custom-call(f32[4,128,128]{2,1,0:T(8,128)S(1)} %cholesky.577), custom_call_target="Cholesky" | custom-call | tf_op jit(solution)/shard_map/vmap(jit(cholesky))/cholesky | solution.py:18
  346.7 39.3 %custom-call.48 = f32[4,1,128,128]{2,3,1,0:T(8,128)S(1)} custom-call(f32[4,1,128,128]{3,2,1,0:T(8,128)S(1)} %select_bitcast_fusion), custom_call_target="InvertDiagBlocksLowerTriangular" | custom-call | tf_op jit(solution)/shard_map/vmap(jit(cholesky))/cholesky | solution.py:18
  389.1 59.6 %custom-call.49 = f32[4,128,128]{2,1,0:T(8,128)S(1)} custom-call(f32[4,128,128]{2,1,0:T(8,128)S(1)} %convolution_subtract_fusion.2), custom_call_target="Cholesky" | custom-call | tf_op jit(solution)/shard_map/vmap(jit(cholesky))/cholesky | solution.py:18
  454.5 79.4 %custom-call.50 = f32[4,2,128,128]{2,3,1,0:T(8,128)S(1)} custom-call(f32[4,2,128,128]{3,2,1,0:T(8,128)} %bitcast.451), custom_call_target="InvertDiagBlocksLowerTriangular" | custom-call | tf_op jit(solution)/shard_map/vmap(jit(_solve_triangular))/triangular_solve | solution.py:20
  550.6 24.3 %custom-call.51 = f32[2,128,128]{2,1,0:T(8,128)S(1)} custom-call(f32[2,128,128]{2,1,0:T(8,128)} %cholesky.580), custom_call_target="Cholesky" | custom-call | tf_op jit(solution)/shard_map/vmap(jit(cholesky))/cholesky | solution.py:18
  577.1 21.5 %custom-call.52 = f32[2,1,128,128]{2,3,1,0:T(8,128)} custom-call(f32[2,1,128,128]{3,2,1,0:T(8,128)} %select_bitcast_fusion.1), custom_call_target="InvertDiagBlocksLowerTriangular" | custom-call | tf_op jit(solution)/shard_map/vmap(jit(cholesky))/cholesky | solution.py:18
  602.5 24.9 %custom-call.53 = f32[2,128,128]{2,1,0:T(8,128)} custom-call(f32[2,128,128]{2,1,0:T(8,128)} %convolution_subtract_fusion.3), custom_call_target="Cholesky" | custom-call | tf_op jit(solution)/shard_map/vmap(jit(cholesky))/cholesky | solution.py:18
  639.6 40.9 %custom-call.54 = f32[2,2,128,128]{2,3,1,0:T(8,128)} custom-call(f32[2,2,128,128]{3,2,1,0:T(8,128)} %bitcast.452), custom_call_target="InvertDiagBlocksLowerTriangular" | custom-call | tf_op jit(solution)/shard_map/vmap(jit(_solve_triangular))/triangular_solve | solution.py:20
  686.5 11.7 %custom-call.67 = f32[1,128,128]{2,1,0:T(8,128)S(1)} custom-call(f32[1,128,128]{2,1,0:T(8,128)S(1)} %cholesky.583), custom_call_target="Cholesky" | custom-call | tf_op jit(solution)/shard_map/vmap(jit(cholesky))/cholesky | solution.py:18
  708.6 12.1 %custom-call.69 = f32[1,128,128]{2,1,0:T(8,128)S(1)} custom-call(f32[1,128,128]{2,1,0:T(8,128)S(1)} %fusion.34), custom_call_target="Cholesky" | custom-call | tf_op jit(solution)/shard_map/vmap(jit(cholesky))/cholesky | solution.py:18
  727.6 19.7 %custom-call.70 = f32[1,2,128,128]{2,3,1,0:T(8,128)S(1)} custom-call(f32[1,2,128,128]{3,2,1,0:T(8,128)S(1)} %bitcast.448), custom_call_target="InvertDiagBlocksLowerTriangular" | custom-call | tf_op jit(solution)/shard_map/vmap(jit(_solve_triangular))/triangular_solve | solution.py:20
  751.4 11.7 %custom-call.71 = f32[1,128,128]{2,1,0:T(8,128)S(1)} custom-call(f32[1,128,128]{2,1,0:T(8,128)S(1)} %cholesky.586), custom_call_target="Cholesky" | custom-call | tf_op jit(solution)/shard_map/vmap(jit(cholesky))/cholesky | solution.py:18
  773.5 11.7 %custom-call.73 = f32[1,128,128]{2,1,0:T(8,128)S(1)} custom-call(f32[1,128,128]{2,1,0:T(8,128)S(1)} %fusion.35), custom_call_target="Cholesky" | custom-call | tf_op jit(solution)/shard_map/vmap(jit(cholesky))/cholesky | solution.py:18
  792.2 19.7 %custom-call.74 = f32[1,2,128,128]{2,3,1,0:T(8,128)S(1)} custom-call(f32[1,2,128,128]{3,2,1,0:T(8,128)S(1)} %bitcast.449), custom_call_target="InvertDiagBlocksLowerTriangular" | custom-call | tf_op jit(solution)/shard_map/vmap(jit(_solve_triangular))/triangular_solve | solution.py:20
  843.8 11.7 %custom-call.77 = f32[1,128,128]{2,1,0:T(8,128)S(1)} custom-call(f32[1,128,128]{2,1,0:T(8,128)S(1)} %fusion.36), custom_call_target="Cholesky" | custom-call | tf_op jit(solution)/shard_map/vmap(jit(cholesky))/cholesky | solution.py:18
  862.5 19.7 %custom-call.78 = f32[1,2,128,128]{2,3,1,0:T(8,128)S(1)} custom-call(f32[1,2,128,128]{3,2,1,0:T(8,128)S(1)} %bitcast.450), custom_call_target="InvertDiagBlocksLowerTriangular" | custom-call | tf_op jit(solution)/shard_map/vmap(jit(_solve_triangular))/triangular_solve | solution.py:20
  915.4 11.7 %custom-call.81 = f32[1,128,128]{2,1,0:T(8,128)S(1)} custom-call(f32[1,128,128]{2,1,0:T(8,128)S(1)} %fusion.37), custom_call_target="Cholesky" | custom-call | tf_op jit(solution)/shard_map/vmap(jit(cholesky))/cholesky | solution.py:18
  934.3 19.7 %custom-call.82 = f32[1,2,128,128]{2,3,1,0:T(8,128)S(1)} custom-call(f32[1,2,128,128]{3,2,1,0:T(8,128)S(1)} %bitcast.447), custom_call_target="InvertDiagBlocksLowerTriangular" | custom-call | tf_op jit(solution)/shard_map/vmap(jit(_solve_triangular))/triangular_solve | solution.py:20
  (223 shorter events, 223.6 us)
Async XLA Ops:
  7.2 1.1 copy-start
  7.2 104.2 %copy-start.11 = (s32[4,5]{1,0:T(4,128)S(1)}, s32[4,5]{1,0:T(4,128)}, u32[]{:S(2)}) copy-start(s32[4,5]{1,0:T(4,128)} %param.8) | copy-start | bytes 244
  7.2 104.2 %all-reduce.5.cloned.1.call-start = ((), (), s32[]{:S(2)}) async-start(), calls=%async_computation | async-start | bytes 2097152 | tf_op jit(solution)/shard_map/psum | solution.py:58
  10.6 199.2 %all-gather.2.cloned.1.call-start = ((), (), s32[]{:S(2)}) async-start(), calls=%async_computation.1 | async-start | bytes 17825792 | tf_op jit(solution)/shard_map/all_gather | solution.py:59
  111.5 235.1 %copy-start.10 = (pred[128,128]{1,0:T(8,128)(4,1)}, pred[128,128]{1,0:T(8,128)(4,1)S(1)}, u32[]{:S(2)}) copy-start(pred[128,128]{1,0:T(8,128)(4,1)S(1)} %iota_compare_fusion.5) | copy-start | bytes 49156
  111.6 337.3 %copy-start.9 = (pred[256,256]{1,0:T(8,128)(4,1)}, pred[256,256]{1,0:T(8,128)(4,1)S(1)}, u32[]{:S(2)}) copy-start(pred[256,256]{1,0:T(8,128)(4,1)S(1)} %iota_compare_fusion.2) | copy-start | bytes 196612
  111.8 422.2 %copy-start.6 = (f32[128,256]{1,0:T(8,128)}, f32[128,256]{1,0:T(8,128)S(1)}, u32[]{:S(2)}) copy-start(f32[128,256]{1,0:T(8,128)S(1)} %get-tuple-element.125) | copy-start | bytes 393220
  111.8 422.8 %copy-start.8 = (f32[128,256]{1,0:T(8,128)}, f32[128,256]{1,0:T(8,128)S(1)}, u32[]{:S(2)}) copy-start(f32[128,256]{1,0:T(8,128)S(1)} %get-tuple-element.124) | copy-start | bytes 393220
  283.6 3.2 copy-start.2
  288.3 9.4 copy-start.4
  298.7 1.0 copy-start.3
  454.5 84.0 %copy-start.13 = (s32[2,2]{1,0:T(2,128)}, s32[2,2]{1,0:T(2,128)S(1)}, u32[]{:S(2)}) copy-start(s32[2,2]{1,0:T(2,128)S(1)} %get-tuple-element.442) | copy-start | bytes 52
  538.5 5.7 copy-start.12
  549.2 0.8 copy-start.5
  629.0 51.5 %copy-start.7 = (f32[128,256]{1,0:T(8,128)S(1)}, f32[128,256]{1,0:T(8,128)}, u32[]{:S(2)}) copy-start(f32[128,256]{1,0:T(8,128)} %copy-done.6) | copy-start | bytes 393220
  686.0 37.5 %copy-start.14 = (s32[2,2]{1,0:T(2,128)S(1)}, s32[2,2]{1,0:T(2,128)}, u32[]{:S(2)}) copy-start(s32[2,2]{1,0:T(2,128)} %get-tuple-element.443) | copy-start | bytes 52
  749.1 1.8 collective-permute-start
  813.5 7.7 collective-permute-start.1
  883.8 9.0 collective-permute-start.2
  893.3 62.7 %copy-start.1 = (bf16[1024,256]{1,0:T(8,128)(2,1)S(1)}, bf16[1024,256]{1,0:T(8,128)(2,1)}, u32[]{:S(2)}) copy-start(bf16[1024,256]{1,0:T(8,128)(2,1)} %param.10) | copy-start | bytes 1572868
Sparse Core Ops, SparseCore 0:
  11.8 99.4 all-reduce.4
  113.2 96.5 all-gather.1
where the time goes:
time: 972 us; the launch traced here: 963 us
  other arithmetic  563 us (58%)
  waiting for transfers between devices  215 us (22%)
  local copies, waits for them, and re-layouts  101 us (10%)
  matrix products  60.2 us (6%)
  between operations  20.7 us (2%)
    another operation x45, other arithmetic, cholqr(): low_factor = jnp.linalg.cholesky(gram_matrix)  359 us
    another operation x14, other arithmetic, cholqr(): jax.scipy.linalg.solve_triangular(low_factor, identity, lower=True)  201 us
    psum x1, waiting for transfers between devices, shards(): sketched = lax.psum(partial_sum.astype(jnp.bfloat16), 'col')  101 us
    all_gather x1, waiting for transfers between devices, shards(): all_sketched = lax.all_gather(sketched, 'row', axis=0, tiled=True)  98 us
    reshape x1, local copies, waits for them, and re-layouts, off_products(): all_sketched.reshape(leaf_total, front_blocks.shape[2], all_sketched.shap...  22.4 us
  transfers between devices with their start and end apart: 5, of which 5 were waited for; matrix products, arithmetic and copies ran while one was open for 0% of the time, Pallas kernels for 0%

commit v1 on v0

v1 whole, which is shorter than its diff:
```python
import math

import jax
import jax.numpy as jnp
from jax import lax
from jax.experimental import pallas as pl
from jax.experimental.pallas import tpu as pltpu
from jax.sharding import PartitionSpec as P

F32 = jnp.float32
BF16 = jnp.bfloat16
HIGHEST = lax.Precision.HIGHEST


def mm(a, b):
    return lax.dot_general(
        a, b, (((1,), (0,)), ((), ())), precision=HIGHEST, preferred_element_type=F32
    )


def mm_t(a, b):
    return lax.dot_general(
        a, b, (((1,), (1,)), ((), ())), precision=HIGHEST, preferred_element_type=F32
    )


def dot_t(a, b):
    return lax.dot_general(a, b, (((1,), (1,)), ((), ())), preferred_element_type=F32)


def factor64(blocks):
    shape = blocks[0].shape
    sub = lax.broadcasted_iota(jnp.int32, shape, 1)
    rows = list(blocks)
    out = []
    for p in range(8):
        base = 64 + 8 * p
        col = {
            q: [jnp.broadcast_to(rows[q][:, :, base + k : base + k + 1], shape) for k in range(8)]
            for q in range(p, 8)
        }
        a = [[None] * 8 for _ in range(8)]
        for k in range(8):
            for i in range(k, 8):
                a[i][k] = jnp.broadcast_to(col[p][k][:, i : i + 1, :], shape)
        r = [jnp.broadcast_to(rows[p][:, j : j + 1, :], shape) for j in range(8)]
        low = {q: [None] * 8 for q in range(p + 1, 8)}
        joined = None
        for j in range(8):
            pivot = a[j][j]
            inv = 1.0 / pivot
            mult = [None] * 8
            for k in range(j + 1, 8):
                mult[k] = a[k][j] * inv
            for k in range(j + 1, 8):
                for i in range(k, 8):
                    a[i][k] = a[i][k] - mult[k] * a[i][j]
                r[k] = r[k] - mult[k] * r[j]
            for q in range(p + 1, 8):
                low[q][j] = col[q][j] * inv
                for k in range(j + 1, 8):
                    col[q][k] = col[q][k] - mult[k] * col[q][j]
            scaled = r[j] * lax.rsqrt(pivot)
            joined = scaled if joined is None else jnp.where(sub == j, scaled, joined)
        out.append(joined)
        for q in range(p + 1, 8):
            terms = [low[q][j] * r[j] for j in range(8)]
            while len(terms) > 1:
                terms = [terms[i] + terms[i + 1] for i in range(0, len(terms), 2)]
            rows[q] = rows[q] - terms[0]
    return out


def inverse64(wide):
    lane = lax.broadcasted_iota(jnp.int32, (64, 128), 1)
    row = lax.broadcasted_iota(jnp.int32, (64, 128), 0)
    eye = (lane == row).astype(F32)
    full = [jnp.where(lane >= 64, w, eye) for w in wide]
    out = factor64([jnp.stack([f[8 * i : 8 * i + 8] for f in full]) for i in range(8)])
    return [jnp.concatenate([o[b] for o in out], axis=0) for b in range(len(wide))]


def inverse128(blocks):
    n = range(len(blocks))
    lane = lax.broadcasted_iota(jnp.int32, (64, 128), 1)
    row = lax.broadcasted_iota(jnp.int32, (64, 128), 0)
    first = inverse64([pltpu.roll(b[:64], 64, 1) for b in blocks])
    first = [jnp.where(lane < 64, f, 0.0) for f in first]
    right = [mm(first[i][:, :64], blocks[i][:64]) for i in n]
    left = [mm_t(blocks[i][64:, :64], first[i][:, :64]) for i in n]
    schur = [blocks[i][64:] - mm(left[i], right[i]) for i in n]
    mixed = [mm(left[i], first[i]) for i in n]
    second = inverse64(schur)
    eye = (lane == row + 64).astype(F32)
    low = [mm(second[i][:, :64], jnp.where(lane < 64, -mixed[i], eye)) for i in n]
    return [jnp.concatenate([first[i], low[i]], axis=0) for i in n]


def inverse256(grams):
    n = range(len(grams))
    first = inverse128([g[0:128, 0:128] for g in grams])
    right = [mm(first[i], grams[i][0:128, 128:256]) for i in n]
    left = [mm_t(grams[i][128:256, 0:128], first[i]) for i in n]
    schur = [grams[i][128:256, 128:256] - mm(left[i], right[i]) for i in n]
    mixed = [mm(left[i], first[i]) for i in n]
    second = inverse128(schur)
    return [(first[i], -mm(second[i], mixed[i]), second[i]) for i in n]


def cholqr_t(z_ts, gram_ref):
    for i, z_t in enumerate(z_ts):
        gram_ref[i] = dot_t(z_t, z_t)
    inverses = inverse256([gram_ref.at[i] for i in range(len(z_ts))])
    out = []
    for z_t, (top, low, bottom) in zip(z_ts, inverses):
        scale = math.sqrt(z_t.shape[1])
        full = jnp.concatenate(
            [
                jnp.concatenate([top, jnp.zeros_like(top)], axis=1),
                jnp.concatenate([low, bottom], axis=1),
            ],
            axis=0,
        ) * scale
        high = full.astype(BF16)
        rest = (full - high.astype(F32)).astype(BF16)
        out.append(
            jnp.dot(high, z_t, preferred_element_type=F32)
            + jnp.dot(rest, z_t, preferred_element_type=F32)
        )
    return out


VMEM = pl.BlockSpec(memory_space=pltpu.MemorySpace.VMEM)
SMEM = pl.BlockSpec(memory_space=pltpu.MemorySpace.SMEM)
PARAMS = pltpu.CompilerParams(vmem_limit_bytes=48 << 20)


def sketch_kernel(x_ref, w_ref, out_ref):
    sources, rows, depth = x_ref.shape
    rank = w_ref.shape[1]
    total = None
    for s in range(sources):
        part = lax.dot_general(
            w_ref[s * depth : (s + 1) * depth, :], x_ref[s],
            (((0,), (1,)), ((), ())), preferred_element_type=F32,
        )
        total = part if total is None else total + part
    pieces = total.astype(BF16).reshape(sources, rank // sources, rows)
    for r in range(out_ref.shape[0]):
        out_ref[r] = pieces


def sketch(x, w, size_rows):
    sources, rows, _ = x.shape
    shape = (size_rows, sources, w.shape[1] // sources, rows)
    return pl.pallas_call(
        sketch_kernel,
        out_shape=jax.ShapeDtypeStruct(shape, BF16),
        in_specs=[VMEM, VMEM],
        out_specs=VMEM,
        compiler_params=PARAMS,
    )(x, w)


def products_kernel(slot_ref, block_ref, front_ref, sk_ref, out_ref, acc_ref):
    leaf, step = pl.program_id(0), pl.program_id(1)
    block = block_ref[leaf, step]
    pieces = front_ref.shape[3] // sk_ref.shape[3]
    sk = jnp.concatenate([sk_ref[block, q] for q in range(pieces)], axis=1)
    part = dot_t(sk, front_ref[0, 0])

    @pl.when(step == 0)
    def _():
        acc_ref[...] = part

    @pl.when(step > 0)
    def _():
        acc_ref[...] += part

    out_ref[0, 0] = acc_ref[...].astype(BF16)


def products(slots, blocks, front, sk):
    leaves, _, size, _ = front.shape
    steps = slots.shape[1]
    cols = sk.shape[2]
    return pl.pallas_call(
        products_kernel,
        out_shape=jax.ShapeDtypeStruct((steps, leaves, cols, size), BF16),
        grid_spec=pltpu.PrefetchScalarGridSpec(
            num_scalar_prefetch=2,
            grid=(leaves, steps),
            in_specs=[
                pl.BlockSpec((1, 1, size, size), lambda m, s, slot, block: (m, slot[m, s], 0, 0)),
                pl.BlockSpec(sk.shape, lambda m, s, slot, block: (0, 0, 0, 0)),
            ],
            out_specs=pl.BlockSpec(
                (1, 1, cols, size), lambda m, s, slot, block: (steps - 1 - s, m, 0, 0)
            ),
            scratch_shapes=[pltpu.VMEM((cols, size), F32)],
        ),
        compiler_params=PARAMS,
    )(slots, blocks, front, sk)


def leaf_kernel(z_ref, basis_ref, basis_t_ref, gram_ref):
    leaves, size = z_ref.shape[1], z_ref.shape[3]
    rank = z_ref.shape[0] * z_ref.shape[2]
    z_ts = [z_ref[:, m].reshape(rank, size) for m in range(leaves)]
    for m, q_t in enumerate(cholqr_t(z_ts, gram_ref)):
        basis_t_ref[m] = q_t.astype(BF16)
        basis_ref[m] = q_t.T.astype(BF16)


def leaf_bases(z):
    sources, leaves, cols, size = z.shape
    rank = sources * cols
    return pl.pallas_call(
        leaf_kernel,
        out_shape=(
            jax.ShapeDtypeStruct((leaves, size, rank), BF16),
            jax.ShapeDtypeStruct((leaves, rank, size), BF16),
        ),
        in_specs=[VMEM],
        out_specs=(VMEM, VMEM),
        scratch_shapes=[pltpu.VMEM((leaves, rank, rank), F32)],
        compiler_params=PARAMS,
    )(z)


def move(stacked, transfer, scale):
    return (dot_t(stacked, transfer) * scale).astype(BF16)


def local_levels_kernel(pick_ref, z_ref, rest_ref, basis_t_ref, out_ref, proj_ref, next_ref, gram_ref):
    leaves, size = z_ref.shape[1], z_ref.shape[3]
    rank = z_ref.shape[0] * z_ref.shape[2]
    levels = pick_ref.shape[1]
    scale = 1.0 / math.sqrt(size)
    for m in range(leaves):
        basis_t = basis_t_ref[m]
        proj_ref[0, m] = move(z_ref[:, m].reshape(rank, size), basis_t, scale)
        for d in range(rest_ref.shape[1]):
            proj_ref[d + 1, m] = move(rest_ref[:, d, m].reshape(rank, size), basis_t, scale)

    def stack1(level, p):
        return jnp.concatenate(
            [proj_ref[pick_ref[m, level - 1], m] for m in (2 * p, 2 * p + 1)], axis=1
        )

    scale = 1.0 / math.sqrt(2 * rank)
    for p, e_t in enumerate(cholqr_t([stack1(1, p) for p in range(leaves // 2)], gram_ref)):
        e_t = e_t.astype(BF16)
        for level in range(2, levels + 1):
            next_ref[level - 2, p] = move(stack1(level, p), e_t, scale)

    def stack2(level):
        return jnp.concatenate([next_ref[level - 2, 0], next_ref[level - 2, 1]], axis=1)

    e_t = cholqr_t([stack2(2)], gram_ref)[0].astype(BF16)
    for level in range(3, levels + 1):
        out_ref[level - 3] = move(stack2(level), e_t, scale)


def local_levels(pick, z, rest, basis_t):
    leaves, rank, _ = basis_t.shape
    levels = pick.shape[1]
    return pl.pallas_call(
        local_levels_kernel,
        out_shape=jax.ShapeDtypeStruct((levels - 2, rank, rank), BF16),
        in_specs=[SMEM, VMEM, VMEM, VMEM],
        out_specs=VMEM,
        scratch_shapes=[
            pltpu.VMEM((rest.shape[1] + 1, leaves, rank, rank), BF16),
            pltpu.VMEM((levels - 1, leaves // 2, rank, rank), BF16),
            pltpu.VMEM((leaves // 2, rank, rank), F32),
        ],
        compiler_params=PARAMS,
    )(pick, z, rest, basis_t)


def pair_t(side_ref, own, partner):
    is_left = side_ref[0] == 0
    left = jnp.where(is_left, own, partner)
    right = jnp.where(is_left, partner, own)
    return jnp.concatenate([left, right], axis=1)


def pair_level_kernel(side_ref, own_ref, partner_ref, out_ref, gram_ref):
    levels, rank, _ = own_ref.shape
    scale = 1.0 / math.sqrt(2 * rank)
    e_t = cholqr_t([pair_t(side_ref, own_ref[0], partner_ref[0])], gram_ref)[0].astype(BF16)
    for level in range(1, levels):
        out_ref[level - 1] = move(pair_t(side_ref, own_ref[level], partner_ref[level]), e_t, scale)


def pair_level(side, own, partner):
    levels, rank, _ = own.shape
    return pl.pallas_call(
        pair_level_kernel,
        out_shape=jax.ShapeDtypeStruct((levels - 1, rank, rank), BF16),
        in_specs=[SMEM, VMEM, VMEM],
        out_specs=VMEM,
        scratch_shapes=[pltpu.VMEM((1, rank, rank), F32)],
        compiler_params=PARAMS,
    )(side, own, partner)


def top_level_kernel(side_ref, own_ref, partner_ref, out_ref, gram_ref, full_ref):
    rows = out_ref.shape[0]
    e_t = cholqr_t([pair_t(side_ref, own_ref[0], partner_ref[0])], gram_ref)[0]
    full_ref[...] = e_t.T
    start = pl.multiple_of(side_ref[1] * rows, rows)
    out_ref[...] = full_ref[pl.ds(start, rows), :].astype(BF16)


def top_level(side, own, partner, rows):
    rank = own.shape[1]
    return pl.pallas_call(
        top_level_kernel,
        out_shape=jax.ShapeDtypeStruct((rows, rank), BF16),
        in_specs=[SMEM, VMEM, VMEM],
        out_specs=VMEM,
        scratch_shapes=[pltpu.VMEM((1, rank, rank), F32), pltpu.VMEM((2 * rank, rank), F32)],
        compiler_params=PARAMS,
    )(side, own, partner)


def plan(block_cols, leaf_ids, top_level):
    level_ids = jnp.arange(top_level, dtype=jnp.int32)
    near = block_cols[:, 2:]
    outside = (
        jnp.right_shift(leaf_ids[:, None, None], level_ids)
        != jnp.right_shift(near[:, :, None], level_ids)
    )
    drop = jnp.sum(outside.astype(jnp.int32), axis=2)
    count = near.shape[1]
    slot_ids = jnp.arange(count, dtype=jnp.int32)
    before = (drop[:, None, :] > drop[:, :, None]) | (
        (drop[:, None, :] == drop[:, :, None]) & (slot_ids[None, None, :] < slot_ids[None, :, None])
    )
    rank = jnp.sum(before.astype(jnp.int32), axis=2)
    chosen = (rank[:, None, :] == slot_ids[None, :, None]).astype(jnp.int32)
    one = jnp.ones_like(near[:, :1])
    slots = jnp.concatenate([one, jnp.sum(chosen * (slot_ids + 2), axis=2)], axis=1)
    blocks = jnp.concatenate([block_cols[:, 1:2], jnp.sum(chosen * near[:, None, :], axis=2)], axis=1)
    pick = jnp.sum((drop[:, None, :] <= level_ids[None, 1:, None]).astype(jnp.int32), axis=2)
    return slots, blocks, pick


def shards(front_blocks, block_cols, samples, sketch_matrix):
    leaf_dev, _, leaf_size, _ = front_blocks.shape
    rank_size = sketch_matrix.shape[1]
    size_rows, size_cols = lax.axis_size("row"), lax.axis_size("col")
    row_index = lax.axis_index("row")
    top = (leaf_dev * size_rows).bit_length() - 1
    leaf_ids = row_index * leaf_dev + jnp.arange(leaf_dev, dtype=jnp.int32)
    slots, blocks, pick = plan(block_cols, leaf_ids, top)

    chunk = samples.shape[0] // size_cols
    mine = lax.all_to_all(samples.reshape(size_cols, chunk, samples.shape[1]), "col", 0, 0)
    pieces = sketch(mine, sketch_matrix, size_rows)
    pieces = pieces.reshape((size_rows * size_cols,) + pieces.shape[2:])
    sk = lax.all_to_all(pieces, ("row", "col"), 0, 0)
    sk = sk.reshape(leaf_dev * size_rows, leaf_size // chunk, sk.shape[1], chunk)

    sums = products(slots, blocks, front_blocks, sk)
    first = jnp.broadcast_to(sums[:1], (size_cols,) + sums.shape[1:])
    rest = lax.all_gather(sums[1:], "col")
    z = lax.all_to_all(first, "col", 0, 0)
    basis, basis_t = leaf_bases(z)
    carried = local_levels(pick, z, rest, basis_t)

    bit = 0
    out_rows = 4 * rank_size // size_rows
    while True:
        partner = lax.ppermute(
            carried, "row", [(s, s ^ (1 << bit)) for s in range(size_rows)]
        )
        side = jnp.stack(
            [jnp.right_shift(row_index, bit) & 1, row_index % (size_rows // 2)]
        ).astype(jnp.int32)
        if carried.shape[0] == 1:
            break
        carried = pair_level(side, carried, partner)
        bit += 1
    top_rows = top_level(side, carried, partner, out_rows)
    return basis.reshape(leaf_dev * leaf_size, rank_size), top_rows


def solution(mesh):
    placed = (P("row", None, None, None), P("row", None), P("row", "col"), P())
    return jax.shard_map(
        shards,
        mesh=mesh,
        in_specs=placed,
        out_specs=(P("row", None), P("row", None)),
        check_vma=False,
    )
```

time: 972 us -> 226 us (0.23)
  other arithmetic: 563 us -> 1.09 us
  waiting for transfers between devices: 215 us -> 61.8 us
  Pallas kernels: 0 us -> 100 us
  local copies, waits for them, and re-layouts: 101 us -> 8.16 us
  matrix products: 60.2 us -> 0 us
  starting transfers between devices: 2.32 us -> 22.1 us
  blocking collectives: 0 us -> 14.9 us
    another operation x60 -> x3, other arithmetic: 560 us -> 0.22 us  [shards(): jnp.stack([jnp.right_shift(row_index, bit) & 1, row_index % (size_rows //...]
    psum x1 -> x0, waiting for transfers between devices: 101 us -> none  [shards(): sketched = lax.psum(partial_sum.astype(jnp.bfloat16), 'col')]
    pallas_call x0 -> x7, Pallas kernels: none -> 100 us  [the longest x1 27.5 us: local_levels(): pl.pallas_call(local_levels_kernel, out_shape=jax.ShapeDtypeStruct((level...]
    all_gather x1, waiting for transfers between devices: 98 us -> 3.87 us  [shards(): rest = lax.all_gather(sums[1:], 'col')]
    all_to_all x0 -> x2, waiting for transfers between devices: none -> 44.7 us  [the longest x1 27.3 us: shards(): sk = lax.all_to_all(pieces, ('row', 'col'), 0, 0)]
    dot_general x20 -> x0, matrix products: 42.1 us -> none  [the longest x1 12.5 us: off_products(): jnp.einsum('nkab,nkbc->nkac', front_blocks, gathered_blocks, preferred_el...]
    another operation x54 -> x0, local copies, waits for them, and re-layouts: 31.7 us -> none  [the longest x30 16.3 us: cholqr(): jax.scipy.linalg.solve_triangular(low_factor, identity, lower=True)]
    reshape x1, local copies, waits for them, and re-layouts: 22.4 us -> 0.06 us  [shards(): samples.reshape(size_cols, chunk, samples.shape[1])]
  transfers between devices with their start and end apart: 5 -> 6, of which waited for: 5 -> 6; matrix products, arithmetic and copies ran while one was open for 0% -> 2% of each run, Pallas kernels for 0% -> 12%
where the time goes in v1:
time: 226 us; the launch traced here: 223 us
  Pallas kernels  100 us (44%)
  waiting for transfers between devices  61.8 us (27%)
  starting transfers between devices  22.1 us (10%)
  blocking collectives  14.9 us (7%)
  between operations  14.3 us (6%)
  local copies, waits for them, and re-layouts  8.16 us (4%)
    pallas_call x1, Pallas kernels, local_levels(): pl.pallas_call(local_levels_kernel, out_shape=jax.ShapeDtypeStruct((level...  27.5 us
    all_to_all x1, waiting for transfers between devices, shards(): sk = lax.all_to_all(pieces, ('row', 'col'), 0, 0)  27.3 us
    pallas_call x1, Pallas kernels, leaf_bases(): pl.pallas_call(leaf_kernel, out_shape=(jax.ShapeDtypeStruct((leaves, size...  25.7 us
    pallas_call x2, Pallas kernels, pair_level(): pl.pallas_call(pair_level_kernel, out_shape=jax.ShapeDtypeStruct((levels...  22.3 us
    all_to_all x1, waiting for transfers between devices, shards(): z = lax.all_to_all(first, 'col', 0, 0)  17.4 us
    all_to_all x1, blocking collectives, shards(): lax.all_to_all(samples.reshape(size_cols, chunk, samples.shape[1]), 'col'...  14.9 us
    ppermute x3, waiting for transfers between devices, shards(): lax.ppermute(carried, 'row', [(s, s ^ 1 << bit) for s in range(size_rows)])  13.2 us
    all_to_all x1, starting transfers between devices, shards(): sk = lax.all_to_all(pieces, ('row', 'col'), 0, 0)  12.3 us
  transfers between devices with their start and end apart: 6, of which 6 were waited for; matrix products, arithmetic and copies ran while one was open for 2% of the time, Pallas kernels for 12%

profile of v1, /device:TPU:1, one launch (start us, length us, event | category | flops | bytes accessed | tf_op | source)
XLA Modules:
  0.0 222.6 jit_solution(6175551741279181395)
XLA Ops:
  7.2 0.9 copy-done
  8.2 14.9 %all_to_all.15 = bf16[16,128,64]{1,2,0:T(8,128)(2,1)S(1)} all-to-all(bf16[16,128,64]{1,2,0:T(8,128)(2,1)S(1)} %copy_bitcast_fusion), channel_id=1, replica_groups=mesh['row'=16,'col'=16] {'col'}, dimensions={0} | all-to-all | bytes 524288 | tf_op jit(solution)/shard_map/all_to_all | solution.py:361
  23.4 1.0 copy-done.2
  24.4 1.5 shard_map.59
  26.0 12.3 %all-to-all-start.1 = ((bf16[256,16,128]{2,1,0:T(8,128)(2,1)}), bf16[256,16,128]{2,1,0:T(8,128)(2,1)S(1)}, u32[]{:S(2)}, u32[]{:S(2)}) async-start(bf16[256,16,128]{2,1,0:T(8,128)(2,1)} %bitcast), calls=%async_computation.1 | async-start | bytes 2097152 | tf_op jit(solution)/shard_map/all_to_all | solution.py:364
  38.4 0.8 slice.15
  41.2 27.3 %all-to-all-done.1 = bf16[256,16,128]{2,1,0:T(8,128)(2,1)S(1)} async-done(((bf16[256,16,128]{2,1,0:T(8,128)(2,1)}), bf16[256,16,128]{2,1,0:T(8,128)(2,1)S(1)}, u32[]{:S(2)}, u32[]{:S(2)}) %all-to-all-start.1) | async-done | bytes 1048608 | tf_op jit(solution)/shard_map/all_to_all | solution.py:364
  68.5 11.7 %shard_map.60 = bf16[4,4,16,512]{3,2,1,0:T(8,128)(2,1)S(1)} custom-call(s32[4,4]{1,0:T(4,128)S(1)} %concatenate.6.slot_ref, s32[4,4]{1,0:T(4,128)S(1)} %pad_add_fusion.block_ref, bf16[4,5,512,512]{3,2,1,0:T(8,128)(2,1)} %front_ref.1, bf16[64,4,16,128]{3,2,1,0:T(8,128)(2,1)S(1)} %bitcast.15), custom_call_target="tpu_custom_call" | custom-call | tf_op jit(solution)/shard_map/pallas_call | solution.py:187
  81.0 1.1 broadcast_in_dim.5
  82.1 4.4 %all-to-all-start.2 = ((bf16[16,4,16,512]{3,2,1,0:T(8,128)(2,1)}), bf16[16,4,16,512]{3,2,1,0:T(8,128)(2,1)S(1)}, u32[]{:S(2)}, u32[]{:S(2)}) async-start(bf16[16,4,16,512]{3,2,1,0:T(8,128)(2,1)} %broadcast_in_dim.5), calls=%async_computation.2 | async-start | bytes 2097152 | tf_op jit(solution)/shard_map/all_to_all | solution.py:370
  86.6 17.4 %all-to-all-done.2.z_ref = bf16[16,4,16,512]{3,2,1,0:T(8,128)(2,1)S(1)} async-done(((bf16[16,4,16,512]{3,2,1,0:T(8,128)(2,1)}), bf16[16,4,16,512]{3,2,1,0:T(8,128)(2,1)S(1)}, u32[]{:S(2)}, u32[]{:S(2)}) %all-to-all-start.2) | async-done | bytes 1048608 | tf_op jit(solution)/shard_map/all_to_all | solution.py:370
  104.0 25.7 %shard_map.61 = (bf16[4,512,256]{2,1,0:T(8,128)(2,1)}, bf16[4,256,512]{2,1,0:T(8,128)(2,1)S(1)}) custom-call(bf16[16,4,16,512]{3,2,1,0:T(8,128)(2,1)S(1)} %all-to-all-done.2.z_ref), custom_call_target="tpu_custom_call" | custom-call | tf_op jit(solution)/shard_map/pallas_call | solution.py:218
  129.7 3.9 %all-gather.3.cloned.1.call-done = bf16[48,4,16,512]{3,2,1,0:T(8,128)(2,1)} async-done(((bf16[3,4,16,512]{3,2,1,0:T(8,128)(2,1)}), bf16[48,4,16,512]{3,2,1,0:T(8,128)(2,1)}) %all-gather.3.cloned.1.call-update) | async-done | bytes 3145744 | tf_op jit(solution)/shard_map/all_gather | solution.py:369
  133.6 1.9 copy-done.1
  135.4 27.5 %shard_map.62.own_ref = bf16[3,256,256]{2,1,0:T(8,128)(2,1)S(1)} custom-call(s32[4,5]{1,0:T(4,128)S(1)} %convert_reduce_fusion.pick_ref, bf16[16,4,16,512]{3,2,1,0:T(8,128)(2,1)S(1)} %all-to-all-done.2.z_ref, bf16[16,3,4,16,512]{4,3,2,1,0:T(8,128)(2,1)S(1)} %bitcast.16, bf16[4,256,512]{2,1,0:T(8,128)(2,1)S(1)} %get-tuple-element.5.basis_t_ref), custom_call_target="tpu_custom_call" | custom-call | tf_op jit(solution)/shard_map/pallas_call | solution.py:268
  162.9 1.1 collective-permute-start
  164.1 1.3 collective-permute-done.partner_ref
  165.3 11.2 %shard_map.63.own_ref = bf16[2,256,256]{2,1,0:T(8,128)(2,1)S(1)} custom-call(s32[2]{0:T(128)S(1)} %pad_add_fusion.3.side_ref, bf16[3,256,256]{2,1,0:T(8,128)(2,1)S(1)} %shard_map.62.own_ref, bf16[3,256,256]{2,1,0:T(8,128)(2,1)S(1)} %collective-permute-done.partner_ref), custom_call_target="tpu_custom_call" | custom-call | tf_op jit(solution)/shard_map/pallas_call | solution.py:299
  176.5 1.8 collective-permute-start.1
  178.4 6.2 %collective-permute-done.1.partner_ref = bf16[2,256,256]{2,1,0:T(8,128)(2,1)S(1)} collective-permute-done((bf16[2,256,256]{2,1,0:T(8,128)(2,1)S(1)}, bf16[2,256,256]{2,1,0:T(8,128)(2,1)S(1)}, u32[]{:S(2)}, u32[]{:S(2)}) %collective-permute-start.1) | collective-permute-done | bytes 262176 | tf_op jit(solution)/shard_map/ppermute | solution.py:377
  184.6 11.1 %shard_map.64.own_ref = bf16[1,256,256]{2,1,0:T(8,128)(2,1)S(1)} custom-call(s32[2]{0:T(128)S(1)} %pad_add_fusion.2.side_ref, bf16[2,256,256]{2,1,0:T(8,128)(2,1)S(1)} %shard_map.63.own_ref, bf16[2,256,256]{2,1,0:T(8,128)(2,1)S(1)} %collective-permute-done.1.partner_ref), custom_call_target="tpu_custom_call" | custom-call | tf_op jit(solution)/shard_map/pallas_call | solution.py:299
  195.7 2.5 %collective-permute-start.2 = (bf16[1,256,256]{2,1,0:T(8,128)(2,1)S(1)}, bf16[1,256,256]{2,1,0:T(8,128)(2,1)S(1)}, u32[]{:S(2)}, u32[]{:S(2)}) collective-permute-start(bf16[1,256,256]{2,1,0:T(8,128)(2,1)S(1)} %shard_map.64.own_ref), channel_id=1, source_target_pairs={{0,64},{16,80},{32,96},{48,112},{64,0},{80,16},{96,32},{112,48},{1... | collective-permute-start | bytes 393224 | tf_op jit(solution)/shard_map/ppermute | solution.py:377
  198.3 5.7 %collective-permute-done.2.partner_ref = bf16[1,256,256]{2,1,0:T(8,128)(2,1)S(1)} collective-permute-done((bf16[1,256,256]{2,1,0:T(8,128)(2,1)S(1)}, bf16[1,256,256]{2,1,0:T(8,128)(2,1)S(1)}, u32[]{:S(2)}, u32[]{:S(2)}) %collective-permute-start.2) | collective-permute-done | bytes 131104 | tf_op jit(solution)/shard_map/ppermute | solution.py:377
  204.0 11.6 %shard_map.65 = bf16[64,256]{1,0:T(8,128)(2,1)} custom-call(s32[2]{0:T(128)S(1)} %pad_add_fusion.1.side_ref, bf16[1,256,256]{2,1,0:T(8,128)(2,1)S(1)} %shard_map.64.own_ref, bf16[1,256,256]{2,1,0:T(8,128)(2,1)S(1)} %collective-permute-done.2.partner_ref), custom_call_target="tpu_custom_call" | custom-call | tf_op jit(solution)/shard_map/pallas_call | solution.py:319
  (30 shorter events, 3.6 us)
Async XLA Ops:
  7.2 1.0 copy-start
  23.4 1.0 copy-start.2
  26.0 42.6 %all-to-all-start.1 = ((bf16[256,16,128]{2,1,0:T(8,128)(2,1)}), bf16[256,16,128]{2,1,0:T(8,128)(2,1)S(1)}, u32[]{:S(2)}, u32[]{:S(2)}) async-start(bf16[256,16,128]{2,1,0:T(8,128)(2,1)} %bitcast), calls=%async_computation.1 | async-start | bytes 2097152 | tf_op jit(solution)/shard_map/all_to_all | solution.py:364
  38.3 95.3 %all-gather.3.cloned.1.call-start = ((), (), s32[]{:S(2)}) async-start(), calls=%async_computation.3 | async-start | bytes 3342336 | tf_op jit(solution)/shard_map/all_gather | solution.py:369
  82.1 21.9 %all-to-all-start.2 = ((bf16[16,4,16,512]{3,2,1,0:T(8,128)(2,1)}), bf16[16,4,16,512]{3,2,1,0:T(8,128)(2,1)S(1)}, u32[]{:S(2)}, u32[]{:S(2)}) async-start(bf16[16,4,16,512]{3,2,1,0:T(8,128)(2,1)} %broadcast_in_dim.5), calls=%async_computation.2 | async-start | bytes 2097152 | tf_op jit(solution)/shard_map/all_to_all | solution.py:370
  133.6 1.9 copy-start.1
  162.9 2.4 %collective-permute-start = (bf16[3,256,256]{2,1,0:T(8,128)(2,1)S(1)}, bf16[3,256,256]{2,1,0:T(8,128)(2,1)S(1)}, u32[]{:S(2)}, u32[]{:S(2)}) collective-permute-start(bf16[3,256,256]{2,1,0:T(8,128)(2,1)S(1)} %shard_map.62.own_ref), channel_id=1, source_target_pairs={{0,16},{16,0},{32,48},{48,32},{64,80},{80,64},{96,112},{112,96},{1... | collective-permute-start | bytes 1179656 | tf_op jit(solution)/shard_map/ppermute | solution.py:377
  176.5 8.0 %collective-permute-start.1 = (bf16[2,256,256]{2,1,0:T(8,128)(2,1)S(1)}, bf16[2,256,256]{2,1,0:T(8,128)(2,1)S(1)}, u32[]{:S(2)}, u32[]{:S(2)}) collective-permute-start(bf16[2,256,256]{2,1,0:T(8,128)(2,1)S(1)} %shard_map.63.own_ref), channel_id=1, source_target_pairs={{0,32},{16,48},{32,0},{48,16},{64,96},{80,112},{96,64},{112,80},{1... | collective-permute-start | bytes 786440 | tf_op jit(solution)/shard_map/ppermute | solution.py:377
  195.7 8.3 %collective-permute-start.2 = (bf16[1,256,256]{2,1,0:T(8,128)(2,1)S(1)}, bf16[1,256,256]{2,1,0:T(8,128)(2,1)S(1)}, u32[]{:S(2)}, u32[]{:S(2)}) collective-permute-start(bf16[1,256,256]{2,1,0:T(8,128)(2,1)S(1)} %shard_map.64.own_ref), channel_id=1, source_target_pairs={{0,64},{16,80},{32,96},{48,112},{64,0},{80,16},{96,32},{112,48},{1... | collective-permute-start | bytes 393224 | tf_op jit(solution)/shard_map/ppermute | solution.py:377
Sparse Core Ops, SparseCore 0:
  81.1 52.4 all-gather.2
